TPU v7x, 32 devices: a whole 2x2x4 slice. The times are simulated.
32 devices in a mesh: poles: 2 (over x), row: 8 (over z, y), col: 2 (over core).
Axes of the slice: x: 2, y: 2, z: 4, core: 2. Of those that a mesh axis runs over, the one named last changes fastest.
Arguments:
- root_inverse: bfloat16 [16384, 8192], P(('poles', 'row'), 'col'), parts along dimension 0, may hold values from -6 to 6
- panels: bfloat16 [4, 1024, 8192], P(('poles', 'col'), None, 'row'), parts along dimension 0, may hold values from -0.1875 to 0.1875
- diag_inverse: bfloat16 [4, 8192, 8192], P(('poles', 'col'), 'row'), parts along dimension 0, may hold values from -6 to 6
- row_lists: int32 [2, 1024], replicated, may hold values from 0 to 8191, as said below
Outputs:
- offdiag_inverse: bfloat16 [4, 1024, 8192], P(('poles', 'col'), None, 'row'), parts along dimension 0
- diag_result: bfloat16 [4, 8192, 8192], P(('poles', 'col'), 'row'), parts along dimension 0
There are 2 independent parts, one for each index of `poles`. A program takes and returns all parts, laid end to end along the dimension named above; an argument that names none is the same for every part. Nothing has to cross between parts.
Inputs may be any that keep to these rules, and one draw needn't show every extreme that they name: `row_lists`: each child's list is strictly increasing and holds the first and the last root row. In each aligned run of 1024 root rows at most 256 of one child's indices fall, and exactly 256 in one run of every list.
All inputs are finite; a program needn't handle non-finite values.
Results may differ from a plain program's by a relative error of at most 0.0055.
Values may be sent and summed in bfloat16 or wider, within the bound.
No kernel may reach another device: no remote copies, remote signals or barrier semaphores. Data moves between devices by JAX's collectives and lax.ppermute only.
A program may use at most 192 MiB of HBM per device.

v0:
```python
import jax
import jax.numpy as jnp
from jax import lax
from jax.sharding import PartitionSpec as P


def pick_listed(root_block, rows, row_index, col_index, most):
    block_rows = root_block.shape[0]
    half_cols = root_block.shape[1]
    listed = rows.shape[0]
    lower = row_index * block_rows
    first = jnp.sum((rows < lower).astype(jnp.int32))
    count = jnp.sum(((rows >= lower) & (rows < lower + block_rows)).astype(jnp.int32))
    offsets = jnp.arange(most, dtype=jnp.int32)
    positions = jnp.clip(first + offsets, 0, listed - 1)
    local_rows = jnp.clip(jnp.take(rows, positions) - lower, 0, block_rows - 1)
    taken = jnp.take(root_block, local_rows, axis=0)
    local_cols = rows - col_index * half_cols
    col_valid = (local_cols >= 0) & (local_cols < half_cols)
    picked = jnp.take(taken, jnp.clip(local_cols, 0, half_cols - 1), axis=1)
    valid = (offsets < count)[:, None] & col_valid[None, :]
    return (jnp.where(valid, picked, jnp.zeros_like(picked)), first, count)


def per_device(root_inverse, panels, diag_inverse, row_lists):
    row_index = lax.axis_index("row")
    col_index = lax.axis_index("col")
    n_rows = lax.axis_size("row")
    listed = row_lists.shape[1]
    most = 2 * listed // n_rows
    block_rows = root_inverse.shape[0]
    first_pick, _, _ = pick_listed(root_inverse, row_lists[0], row_index, col_index, most)
    second_pick, _, _ = pick_listed(root_inverse, row_lists[1], row_index, col_index, most)
    both_picks = jnp.stack([first_pick, second_pick]).astype(jnp.float32)
    own_rows = (
        lax.psum_scatter(both_picks.astype(jnp.bfloat16), "col", scatter_dimension=0, tiled=True)
        .astype(jnp.float32)[0]
        .astype(jnp.bfloat16)
    )
    child_rows = lax.dynamic_index_in_dim(row_lists, col_index, 0, keepdims=False)
    gathered = lax.all_gather(own_rows, "row", axis=0, tiled=True)
    owners = child_rows // block_rows
    bounds = jnp.arange(n_rows, dtype=jnp.int32) * block_rows
    starts = jnp.sum((child_rows[None, :] < bounds[:, None]).astype(jnp.int32), axis=1)
    ranking = jnp.arange(listed, dtype=jnp.int32) - jnp.take(starts, owners)
    root_part = jnp.take(gathered, owners * most + ranking, axis=0)
    panel = panels[0]
    offdiag = (-jnp.dot(root_part, panel, preferred_element_type=jnp.float32)).astype(jnp.bfloat16)
    diag_rows = diag_inverse[0]
    update_rows = lax.dot_general(
        offdiag,
        lax.all_gather(panel, "row", axis=1, tiled=True),
        (((0,), (0,)), ((), ())),
        preferred_element_type=jnp.float32,
    )
    block_mine = (diag_rows.astype(jnp.float32) - update_rows).astype(jnp.bfloat16)
    partner = lax.all_to_all(block_mine, "row", split_axis=1, concat_axis=0, tiled=True)
    result = ((block_mine.astype(jnp.float32) + partner.T.astype(jnp.float32)) * 0.5).astype(
        jnp.bfloat16
    )
    return (offdiag[None], result[None])


def solution(mesh):
    placed = (
        P(("poles", "row"), "col"),
        P(("poles", "col"), None, "row"),
        P(("poles", "col"), "row", None),
        P(),
    )
    return jax.shard_map(
        per_device,
        mesh=mesh,
        in_specs=placed,
        out_specs=(P(("poles", "col"), None, "row"), P(("poles", "col"), "row", None)),
        check_vma=False,
    )
```

profile of v0, /device:TPU:0, one launch (start us, length us, event | category | flops | bytes accessed | tf_op | source)
XLA Modules:
  0.0 845.1 jit_solution(16834829791201554010)
XLA Ops:
  7.2 0.8 and_reduce_fusion.1
  8.0 0.8 constant_dynamic-slice_fusion
  8.9 0.8 convert_reduce_fusion.2
  11.5 0.7 compare_select_fusion.18
  12.2 1.4 gather_fusion.1
  13.6 0.7 compare_and_fusion.4
  14.3 1.4 gather_fusion.4
  16.4 8.3 gather_fusion.2
  24.8 1.6 broadcast_select_fusion.1
  26.3 3.3 copy.19
  29.6 9.7 %gather_fusion.5 = bf16[256,4096]{1,0:T(8,128)(2,1)} fusion(bf16[1024,4096]{1,0:T(8,128)(2,1)} %param.10, s32[1024]{0:T(1024)S(1)} %pad_clamp_fusion), kind=kCustom, calls=%fused_computation.4.clone | custom fusion | bytes 4195328 | tf_op jit(solution)/shard_map/jit(_take)/gather | solution.py:17
  39.3 3.2 broadcast_select_fusion
  42.4 4.1 copy.20
  46.5 3.9 gather_fusion.3
  50.4 5.5 gather_fusion.6
  56.7 1.1 pad_maximum_fusion
  57.8 11.2 %reduce-scatter.2.cloned.1.call-done = bf16[1,256,1024]{1,2,0:T(8,128)(2,1)} async-done(((bf16[2,256,1024]{1,2,0:T(8,128)(2,1)}), bf16[1,256,1024]{1,2,0:T(8,128)(2,1)}) %reduce-scatter.2.cloned.1.call-update) | async-done | bytes 524304 | tf_op jit(solution)/shard_map/reduce_scatter | solution.py:36
  69.1 0.7 all-gather.7.cloned.1.call-update
  70.0 0.7 fusion.19
  70.6 4.3 compare_select_fusion.2
  75.0 0.7 compare_and_fusion.2
  75.7 71.2 %all-gather.5.cloned.1.call-done = bf16[1,2048,1024]{1,2,0:T(8,128)(2,1)} async-done(((bf16[1,256,1024]{1,2,0:T(8,128)(2,1)}), bf16[1,2048,1024]{1,2,0:T(8,128)(2,1)}) %all-gather.5.cloned.1.call-update) | async-done | bytes 4194320 | tf_op jit(solution)/shard_map/all_gather | solution.py:41
  146.9 6.4 copy.21
  153.3 8.4 gather_fusion
  161.8 5.3 negate_convert_fusion
  167.1 207.5 %all-gather.7.cloned.1.call-done = bf16[1,1024,8192]{2,1,0:T(8,128)(2,1)} async-done(((bf16[1,1024,1024]{2,1,0:T(8,128)(2,1)}), bf16[1,1024,8192]{2,1,0:T(8,128)(2,1)}) %all-gather.7.cloned.1.call-update) | async-done | bytes 16777232 | tf_op jit(solution)/shard_map/all_gather | solution.py:52
  374.6 26.1 %fusion = bf16[1024,8192]{1,0:T(8,128)(2,1)} fusion(bf16[1024,1024]{1,0:T(8,128)(2,1)} %negate_convert_fusion, bf16[1,1024,8192]{2,1,0:T(8,128)(2,1)} %param.12, bf16[1,1024,8192]{2,1,0:T(8,128)(2,1)} %all-gather.7.cloned.1.call-done), kind=kOutput, calls=%fused_computation.8 | convolution fusion | flops 17205035008 | bytes 52428800 | tf_op jit(solution)/shard_map/dot_general | solution.py:50
  400.7 8.1 copy.27
  408.8 365.4 %all_to_all.13 = bf16[1024,8,1024]{2,0,1:T(8,128)(2,1)S(1)} all-to-all(bf16[1024,8,1024]{2,0,1:T(8,128)(2,1)S(1)} %bitcast.67), channel_id=1, replica_groups=mesh['poles'=2,'row'=8,'col'=2] {'row'}, dimensions={1} | all-to-all | bytes 33554432 | tf_op jit(solution)/shard_map/all_to_all | solution.py:57
  774.2 11.2 %convert_element_type.71 = f32[1024,8,1024]{2,0,1:T(8,128)} convert(bf16[1024,8,1024]{2,0,1:T(8,128)(2,1)S(1)} %all_to_all.13) | non-fusion elementwise | flops 8388608 | bytes 50331648 | tf_op jit(solution)/shard_map/convert_element_type | solution.py:58
  785.4 31.1 %copy.24 = f32[8192,1024]{0,1:T(8,128)} copy(f32[8192,1024]{1,0:T(8,128)} %bitcast.66) | data formatting | bytes 67108864 | tf_op jit(solution)/shard_map/convert_element_type | solution.py:58
  816.5 22.1 %fusion.3 = bf16[1,1024,8192]{2,1,0:T(8,128)(2,1)} fusion(f32[8192,1024]{0,1:T(8,128)} %copy.24, bf16[1024,8192]{1,0:T(8,128)(2,1)} %fusion), kind=kLoop, calls=%fused_computation.12 | loop fusion | flops 33554432 | bytes 67108864 | tf_op jit(solution)/shard_map/broadcast_in_dim | solution.py:61
  (21 shorter events, 3.6 us)
Async XLA Ops:
  7.2 61.8 %reduce-scatter.2.cloned.1.call-start = ((), (), s32[]{:S(2)}) async-start(), calls=%async_computation.2 | async-start | bytes 1572864 | tf_op jit(solution)/shard_map/reduce_scatter | solution.py:36
  57.7 89.2 %all-gather.5.cloned.1.call-start = ((), (), s32[]{:S(2)}) async-start(), calls=%async_computation.3 | async-start | bytes 4718592 | tf_op jit(solution)/shard_map/all_gather | solution.py:41
  69.0 305.6 %all-gather.7.cloned.1.call-start = ((), (), s32[]{:S(2)}) async-start(), calls=%async_computation.4 | async-start | bytes 18874368 | tf_op jit(solution)/shard_map/all_gather | solution.py:52
Sparse Core Ops, SparseCore 0:
  57.9 11.1 reduce-scatter.1
  71.1 75.8 all-gather.4
  149.1 225.4 all-gather.6
where the time goes:
time: 846 us; the launch traced here: 845 us
  blocking collectives  365 us (43%)
  waiting for transfers between devices  291 us (34%)
  local copies, waits for them, and re-layouts  93 us (11%)
  other arithmetic  50.6 us (6%)
  matrix products  31.4 us (4%)
  between operations  13.9 us (2%)
    all_to_all x1, blocking collectives, per_device(): lax.all_to_all(block_mine, 'row', split_axis=1, concat_axis=0, tiled=True)  365 us
    all_gather x1, waiting for transfers between devices, per_device(): lax.all_gather(panel, 'row', axis=1, tiled=True)  208 us
    all_gather x1, waiting for transfers between devices, per_device(): gathered = lax.all_gather(own_rows, 'row', axis=0, tiled=True)  71.2 us
    convert_element_type x1, local copies, waits for them, and re-layouts, per_device(): partner.T.astype(jnp.float32)  31.1 us
    dot_general x1, matrix products, per_device(): lax.dot_general(offdiag, lax.all_gather(panel, 'row', axis=1, tiled=True)...  26.1 us
    broadcast_in_dim x1, other arithmetic, per_device(): return (offdiag[None], result[None])  22.1 us
    gather x2, local copies, waits for them, and re-layouts, pick_listed(): taken = jnp.take(root_block, local_rows, axis=0)  18 us
  transfers between devices with their start and end apart: 3, of which 3 were waited for; matrix products, arithmetic and copies ran while one was open for 3% of the time, Pallas kernels for 0%

commit v1 on v0

v1 whole, which is shorter than its diff:
```python
import functools

import jax
import jax.numpy as jnp
from jax import lax
from jax.experimental import pallas as pl
from jax.experimental.pallas import tpu as pltpu
from jax.sharding import PartitionSpec as P

VMEM_BYTES = 48 * 1024 * 1024


def pair_kernel(where, left, right, mine, theirs, *rest, send):
    result, out = (rest[-2], rest[-1]) if send else (rest[-1], None)
    total = jnp.dot(left[...], right[...], preferred_element_type=jnp.float32)
    swapped = theirs[...].astype(jnp.float32).T
    value = total + 0.5 * (mine[...].astype(jnp.float32) + swapped)
    result[...] = value.astype(jnp.bfloat16)
    if send:
        out[...] = value.T.astype(jnp.bfloat16)


def pair_block(where, left, right, diag, theirs, result, send):
    size, depth = left.shape
    tile = min(256, size)
    steps = size // tile
    shape = jax.ShapeDtypeStruct(diag.shape, jnp.bfloat16)
    in_specs = [
        pl.BlockSpec((size, depth), lambda t, w: (0, 0)),
        pl.BlockSpec((depth, tile), lambda t, w: (0, t)),
        pl.BlockSpec((size, tile), lambda t, w: (0, w[0] * steps + t)),
        pl.BlockSpec((tile, size), lambda t, w: (t, 0)),
    ]
    operands = [where, left, right, diag, theirs]
    if theirs is diag:
        in_specs[3] = pl.BlockSpec((tile, size), lambda t, w: (t, w[0]))
    aliases = {}
    if result is not None:
        in_specs.append(pl.BlockSpec(memory_space=pl.ANY))
        aliases = {len(operands): 0}
        operands.append(result)
    out_specs = [pl.BlockSpec((size, tile), lambda t, w: (0, w[0] * steps + t))]
    out_shape = [shape]
    if send:
        out_specs.append(pl.BlockSpec((tile, size), lambda t, w: (t, 0)))
        out_shape.append(jax.ShapeDtypeStruct((size, size), jnp.bfloat16))
    moved = 2 * (2 * size * depth + (4 if send else 3) * size * size)
    return pl.pallas_call(
        functools.partial(pair_kernel, send=send),
        grid_spec=pltpu.PrefetchScalarGridSpec(
            num_scalar_prefetch=1, grid=(steps,), in_specs=in_specs, out_specs=out_specs
        ),
        out_shape=out_shape,
        input_output_aliases=aliases,
        compiler_params=pltpu.CompilerParams(vmem_limit_bytes=VMEM_BYTES),
        cost_estimate=pl.CostEstimate(
            flops=2 * size * size * depth, bytes_accessed=moved, transcendentals=0
        ),
        name="pair_send" if send else "pair_keep",
    )(*operands)


def place_kernel(where, arrived, current, out):
    keep = where[1] == 1

    @pl.when(keep)
    def _():
        out[...] = current[...]

    @pl.when(jnp.logical_not(keep))
    def _():
        out[...] = arrived[...]


def place_block(where, arrived, result):
    size = arrived.shape[0]
    tile = min(256, size)
    spec = pl.BlockSpec((tile, size), lambda t, w: (t, w[0]))
    return pl.pallas_call(
        place_kernel,
        grid_spec=pltpu.PrefetchScalarGridSpec(
            num_scalar_prefetch=1,
            grid=(size // tile,),
            in_specs=[pl.BlockSpec((tile, size), lambda t, w: (t, 0)), spec],
            out_specs=spec,
        ),
        out_shape=jax.ShapeDtypeStruct(result.shape, result.dtype),
        input_output_aliases={2: 0},
        compiler_params=pltpu.CompilerParams(vmem_limit_bytes=VMEM_BYTES),
        cost_estimate=pl.CostEstimate(
            flops=0, bytes_accessed=6 * size * size, transcendentals=0
        ),
        name="place",
    )(where, arrived, result)


def pick_listed(root_block, rows, row_index, col_index, most):
    block_rows, half_cols = root_block.shape
    lower = row_index * block_rows
    first = jnp.sum((rows < lower).astype(jnp.int32))
    padded = jnp.concatenate([rows, jnp.full((most,), jnp.iinfo(jnp.int32).max, jnp.int32)])
    local_rows = lax.dynamic_slice_in_dim(padded, first, most) - lower
    take_rows = (
        local_rows[:, None] == lax.broadcasted_iota(jnp.int32, (most, block_rows), 1)
    ).astype(jnp.bfloat16)
    taken = jnp.dot(take_rows, root_block, preferred_element_type=jnp.float32)
    local_cols = rows - col_index * half_cols
    take_cols = (
        local_cols[None, :] == lax.broadcasted_iota(jnp.int32, (half_cols, rows.shape[0]), 0)
    ).astype(jnp.bfloat16)
    picked = jnp.dot(
        taken.astype(jnp.bfloat16), take_cols, preferred_element_type=jnp.float32
    )
    return picked.astype(jnp.bfloat16)


def per_device(root_inverse, panels, diag_inverse, row_lists):
    row_index = lax.axis_index("row")
    col_index = lax.axis_index("col")
    n_rows = lax.axis_size("row")
    n_cols = lax.axis_size("col")
    half = n_rows // 2
    listed = row_lists.shape[1]
    most = 2 * listed // n_rows
    block_rows = root_inverse.shape[0]
    panel = panels[0]
    diag = diag_inverse[0]
    size = diag.shape[0]
    computes = (row_index // half == col_index).astype(jnp.int32)

    def side(row, col):
        return row // half == col

    def swap(value, step, sender):
        pairs = [
            (row * n_cols + col, (row ^ step) * n_cols + col)
            for row in range(n_rows)
            for col in range(n_cols)
            if sender is None or side(row, col) == sender
        ]
        return lax.ppermute(value, ("row", "col"), pairs)

    def wanted(step):
        return lax.dynamic_slice_in_dim(diag, (row_index ^ step) * size, size, 1)

    held = {0: panel}
    held[half] = swap(panel, half, False)
    step = half // 2
    while step >= 1:
        for slot in sorted(held, reverse=True):
            held[slot ^ step] = swap(held[slot], step, True if slot >= half else None)
        step //= 2

    theirs = {0: diag}
    for step in range(n_rows - 1, 0, -1):
        theirs[step] = swap(wanted(step), step, False if step >= half else None)

    other_rows = lax.dynamic_index_in_dim(row_lists, 1 - col_index, 0, keepdims=False)
    child_rows = lax.dynamic_index_in_dim(row_lists, col_index, 0, keepdims=False)
    for_other = pick_listed(root_inverse, other_rows, row_index, col_index, most)
    from_other = lax.ppermute(for_other, "col", [(0, 1), (1, 0)])
    own = pick_listed(root_inverse, child_rows, row_index, col_index, most) + from_other
    pieces = {0: own}
    step = half
    while step >= 1:
        for slot in list(pieces):
            pieces[slot ^ step] = swap(pieces[slot], step, None)
        step //= 2
    stacked = jnp.concatenate([pieces[slot] for slot in range(n_rows)], axis=0)
    owners = child_rows // block_rows
    bounds = jnp.arange(n_rows, dtype=jnp.int32) * block_rows
    starts = jnp.sum((child_rows[None, :] < bounds[:, None]).astype(jnp.int32), axis=1)
    begun = jnp.sum(
        jnp.where(owners[:, None] == jnp.arange(n_rows, dtype=jnp.int32)[None, :], starts[None, :], 0),
        axis=1,
    )
    ranking = jnp.arange(listed, dtype=jnp.int32) - begun
    place = (owners ^ row_index) * most + ranking
    chosen = (
        place[:, None] == lax.broadcasted_iota(jnp.int32, (listed, n_rows * most), 1)
    ).astype(jnp.bfloat16)
    root_part = jnp.dot(chosen, stacked, preferred_element_type=jnp.float32).astype(jnp.bfloat16)

    offdiag = (-jnp.dot(root_part, panel, preferred_element_type=jnp.float32)).astype(jnp.bfloat16)
    straight = lax.dot_general(
        panel, root_part, (((0,), (1,)), ((), ())), preferred_element_type=jnp.float32
    )
    crossed = lax.dot_general(
        panel, root_part, (((0,), (0,)), ((), ())), preferred_element_type=jnp.float32
    )
    left = (0.5 * (straight + crossed)).astype(jnp.bfloat16)

    result = None
    returned = {}
    order = list(range(half)) + list(range(half, n_rows))
    for step in order:
        where = jnp.stack([row_index ^ step, computes])
        outs = pair_block(where, left, held[step], diag, theirs[step], result, step >= half)
        result = outs[0]
        if step >= half:
            returned[step] = swap(outs[1], step, True)
    for step in range(half, n_rows):
        where = jnp.stack([row_index ^ step, computes])
        result = place_block(where, returned[step], result)
    return (offdiag[None], result[None])


def solution(mesh):
    placed = (
        P(("poles", "row"), "col"),
        P(("poles", "col"), None, "row"),
        P(("poles", "col"), "row", None),
        P(),
    )

    return jax.shard_map(
        per_device,
        mesh=mesh,
        in_specs=placed,
        out_specs=(P(("poles", "col"), None, "row"), P(("poles", "col"), "row", None)),
        check_vma=False,
    )
```

time: 846 us -> 674 us (0.80)
  the two profiles are of different devices: /device:TPU:0 before, /device:TPU:18 now
where the time goes in v1:
time: 674 us; the launch traced here: 672 us
  waiting for transfers between devices  471 us (70%)
  Pallas kernels  71 us (11%)
  starting transfers between devices  57.3 us (9%)
  matrix products  35.5 us (5%)
  local copies, waits for them, and re-layouts  26.1 us (4%)
    ppermute x25, waiting for transfers between devices, swap(): return lax.ppermute(value, ('row', 'col'), pairs)  471 us
    ppermute x25, starting transfers between devices, swap(): return lax.ppermute(value, ('row', 'col'), pairs)  57.2 us
    pallas_call x8, Pallas kernels, pair_block(): pl.pallas_call(functools.partial(pair_kernel, send=send), grid_spec=pltpu...  53.6 us
    dot_general x2, matrix products, pick_listed(): jnp.dot(taken.astype(jnp.bfloat16), take_cols, preferred_element_type=jnp...  18.9 us
    pallas_call x4, Pallas kernels, place_block(): pl.pallas_call(place_kernel, grid_spec=pltpu.PrefetchScalarGridSpec(num_s...  17.3 us
  transfers between devices with their start and end apart: 26, of which 13 were waited for; matrix products, arithmetic and copies ran while one was open for 7% of the time, Pallas kernels for 10%

profile of v1, /device:TPU:18, one launch (start us, length us, event | category | flops | bytes accessed | tf_op | source)
XLA Modules:
  0.0 672.3 jit_solution(350366572967500352)
XLA Ops:
  4.4 9.0 %fusion.9 = bf16[256,1024]{1,0:T(8,128)(2,1)S(1)} fusion(s32[1024]{0:T(1024)S(1)} %bitcast.64, bf16[1024,4096]{1,0:T(8,128)(2,1)} %param.4, s32[256]{0:T(256)S(1)} %fusion.19), kind=kOutput, calls=%fused_computation.23 | convolution fusion | flops 4300734464 | bytes 8918016 | tf_op jit(solution)/shard_map/dot_general | solution.py:111
  15.5 10.0 %constant_dynamic-update-slice_fusion.7 = (bf16[2048,1024]{1,0:T(8,128)(2,1)}, bf16[256,1024]{1,0:T(8,128)(2,1)}) fusion(bf16[256,1024]{1,0:T(8,128)(2,1)S(1)} %collective-permute-done, s32[1024]{0:T(1024)S(1)} %bitcast.63, bf16[1024,4096]{1,0:T(8,128)(2,1)} %param.4, s32[256]{0:T(256)S(1)} %fusion.18), kind=kOutput, calls=%fused_computation.40 | convolution fusion | flops 4301783040 | bytes 9966592 | tf_op jit(solution)/shard_map/dot_general | solution.py:111
  27.4 11.1 %dynamic-slice_bitcast_fusion = (bf16[1024,1024]{1,0:T(8,128)(2,1)}, bf16[1024,1024]{1,0:T(8,128)(2,1)}, bf16[1024,1024]{1,0:T(8,128)(2,1)}, bf16[1024,1024]{1,0...) fusion(bf16[1,1024,8192]{2,1,0:T(8,128)(2,1)} %param.6, ...), kind=kLoop, calls=%fused_computation.15 | loop fusion | bytes 29360156 | tf_op jit(solution)/shard_map/dynamic_slice | solution.py:144
  42.1 7.1 %collective-permute-done.2 = bf16[256,1024]{1,0:T(8,128)(2,1)S(1)} collective-permute-done((bf16[256,1024]{1,0:T(8,128)(2,1)}, bf16[256,1024]{1,0:T(8,128)(2,1)S(1)}, u32[]{:S(2)}, u32[]{:S(2)}) %collective-permute-start.2) | collective-permute-done | bytes 524320 | tf_op jit(solution)/shard_map/ppermute | solution.py:141
  52.8 90.7 %collective-permute-done.1 = bf16[256,1024]{1,0:T(8,128)(2,1)S(1)} collective-permute-done((bf16[256,1024]{1,0:T(8,128)(2,1)}, bf16[256,1024]{1,0:T(8,128)(2,1)S(1)}, u32[]{:S(2)}, u32[]{:S(2)}) %collective-permute-start.1) | collective-permute-done | bytes 524320 | tf_op jit(solution)/shard_map/ppermute | solution.py:141
  143.9 10.8 %collective-permute-done.3 = bf16[256,1024]{1,0:T(8,128)(2,1)S(1)} collective-permute-done((bf16[256,1024]{1,0:T(8,128)(2,1)S(1)}, bf16[256,1024]{1,0:T(8,128)(2,1)S(1)}, u32[]{:S(2)}, u32[]{:S(2)}) %collective-permute-start.3) | collective-permute-done | bytes 524320 | tf_op jit(solution)/shard_map/ppermute | solution.py:141
  154.7 5.8 collective-permute-start.8
  160.5 4.4 collective-permute-done.5
  166.3 56.5 %collective-permute-done.6 = bf16[256,1024]{1,0:T(8,128)(2,1)} collective-permute-done((bf16[256,1024]{1,0:T(8,128)(2,1)S(1)}, bf16[256,1024]{1,0:T(8,128)(2,1)}, u32[]{:S(2)}, u32[]{:S(2)}) %collective-permute-start.6) | collective-permute-done | bytes 524320 | tf_op jit(solution)/shard_map/ppermute | solution.py:141
  224.7 8.0 %collective-permute-done.7 = bf16[256,1024]{1,0:T(8,128)(2,1)S(1)} collective-permute-done((bf16[256,1024]{1,0:T(8,128)(2,1)}, bf16[256,1024]{1,0:T(8,128)(2,1)S(1)}, u32[]{:S(2)}, u32[]{:S(2)}) %collective-permute-start.7) | collective-permute-done | bytes 524320 | tf_op jit(solution)/shard_map/ppermute | solution.py:141
  236.2 7.8 %collective-permute-start.15 = (bf16[1024,1024]{1,0:T(8,128)(2,1)}, bf16[1024,1024]{1,0:T(8,128)(2,1)}, u32[]{:S(2)}, u32[]{:S(2)}) collective-permute-start(bf16[1024,1024]{1,0:T(8,128)(2,1)} %get-tuple-element.24), channel_id=1, source_target_pairs={{1,9},{3,11},{5,13},{7,15},{8,0},{10,2},{12,4},{14,6},{17,25},{19,... | collective-permute-start | bytes 6291464 | tf_op jit(solution)/shard_map/ppermute | solution.py:141
  255.7 7.1 %fusion.8 = bf16[1024,1024]{1,0:T(8,128)(2,1)S(1)} fusion(bf16[2048,1024]{1,0:T(8,128)(2,1)} %constant_dynamic-update-slice_fusion, s32[1024]{0:T(1024)S(1)} %get-tuple-element.31), kind=kOutput, calls=%fused_computation.22 | convolution fusion | flops 4298113024 | bytes 6295552 | tf_op jit(solution)/shard_map/dot_general | solution.py:182
  262.8 41.3 %collective-permute-done.19.theirs = bf16[1024,1024]{1,0:T(8,128)(2,1)} collective-permute-done((bf16[1024,1024]{1,0:T(8,128)(2,1)}, bf16[1024,1024]{1,0:T(8,128)(2,1)}, u32[]{:S(2)}, u32[]{:S(2)}) %collective-permute-start.19) | collective-permute-done | bytes 2097184 | tf_op jit(solution)/shard_map/ppermute | solution.py:141
  304.1 9.1 %collective-permute-start.14 = (bf16[1024,1024]{1,0:T(8,128)(2,1)}, bf16[1024,1024]{1,0:T(8,128)(2,1)}, u32[]{:S(2)}, u32[]{:S(2)}) collective-permute-start(bf16[1024,1024]{1,0:T(8,128)(2,1)} %get-tuple-element.25), channel_id=1, source_target_pairs={{1,11},{3,9},{5,15},{7,13},{8,2},{10,0},{12,6},{14,4},{17,27},{19,... | collective-permute-start | bytes 6291464 | tf_op jit(solution)/shard_map/ppermute | solution.py:141
  313.2 58.3 %collective-permute-done.18.theirs = bf16[1024,1024]{1,0:T(8,128)(2,1)} collective-permute-done((bf16[1024,1024]{1,0:T(8,128)(2,1)}, bf16[1024,1024]{1,0:T(8,128)(2,1)}, u32[]{:S(2)}, u32[]{:S(2)}) %collective-permute-start.18) | collective-permute-done | bytes 2097184 | tf_op jit(solution)/shard_map/ppermute | solution.py:141
  371.5 5.5 collective-permute-start.12
  383.3 5.3 copy.19
  393.3 5.2 fusion.7.left
  398.5 6.6 pair_keep.4.rest_0_
  405.1 6.6 pair_keep.5.rest_0_
  411.7 6.6 pair_keep.6.rest_0_
  418.3 6.6 pair_keep.7.rest_0_
  424.9 6.7 pair_send.4
  432.9 6.7 pair_send.5
  440.9 127.6 %collective-permute-done.12.theirs = bf16[1024,1024]{1,0:T(8,128)(2,1)} collective-permute-done((bf16[1024,1024]{1,0:T(8,128)(2,1)}, bf16[1024,1024]{1,0:T(8,128)(2,1)}, u32[]{:S(2)}, u32[]{:S(2)}) %collective-permute-start.12) | collective-permute-done | bytes 2097184 | tf_op jit(solution)/shard_map/ppermute | solution.py:141
  568.5 7.2 %pair_send.6 = (bf16[1024,8192]{1,0:T(8,128)(2,1)}, bf16[1024,1024]{1,0:T(8,128)(2,1)}) custom-call(s32[2]{0:T(128)S(1)} %pad_add_fusion.1.where, bf16[1024,1024]{1,0:T(8,128)(2,1)S(1)} %fusion.7.left, bf16[1024,1024]{1,0:T(8,128)(2,1)} %collective-permute-done.9.right, bf16[1024,8192]{1,0:T(8,128)(2,1)} %bitcast.55, ...), custom_call_target="tpu_custom_call", output_to_operand_aliasing={{0}: (5, {})} | custom-call | flops 2147483648 | bytes 12582912 | tf_op jit(solution)/shard_map/pair_send/pallas_call | solution.py:48
  576.9 36.5 %collective-permute-done.11.theirs = bf16[1024,1024]{1,0:T(8,128)(2,1)} collective-permute-done((bf16[1024,1024]{1,0:T(8,128)(2,1)}, bf16[1024,1024]{1,0:T(8,128)(2,1)}, u32[]{:S(2)}, u32[]{:S(2)}) %collective-permute-start.11) | collective-permute-done | bytes 2097184 | tf_op jit(solution)/shard_map/ppermute | solution.py:141
  613.4 6.7 pair_send.7
  625.5 4.3 place.4.current
  629.8 4.3 place.5.current
  634.2 10.5 %collective-permute-done.23.arrived = bf16[1024,1024]{1,0:T(8,128)(2,1)S(1)} collective-permute-done((bf16[1024,1024]{1,0:T(8,128)(2,1)}, bf16[1024,1024]{1,0:T(8,128)(2,1)S(1)}, u32[]{:S(2)}, u32[]{:S(2)}) %collective-permute-start.23) | collective-permute-done | bytes 2097184 | tf_op jit(solution)/shard_map/ppermute | solution.py:141
  648.9 19.1 %collective-permute-done.22.arrived = bf16[1024,1024]{1,0:T(8,128)(2,1)S(1)} collective-permute-done((bf16[1024,1024]{1,0:T(8,128)(2,1)S(1)}, bf16[1024,1024]{1,0:T(8,128)(2,1)S(1)}, u32[]{:S(2)}, u32[]{:S(2)}) %collective-permute-start.22) | collective-permute-done | bytes 2097184 | tf_op jit(solution)/shard_map/ppermute | solution.py:141
  (75 shorter events, 58.9 us)
Async XLA Ops:
  13.4 2.1 collective-permute-start
  25.5 14.6 %copy-start = (bf16[1,1024,1024]{2,1,0:T(8,128)(2,1)S(1)}, bf16[1,1024,1024]{2,1,0:T(8,128)(2,1)}, u32[]{:S(2)}) copy-start(bf16[1,1024,1024]{2,1,0:T(8,128)(2,1)} %param.5) | copy-start | bytes 6291460
  25.5 23.7 %collective-permute-start.2 = (bf16[256,1024]{1,0:T(8,128)(2,1)}, bf16[256,1024]{1,0:T(8,128)(2,1)S(1)}, u32[]{:S(2)}, u32[]{:S(2)}) collective-permute-start(bf16[256,1024]{1,0:T(8,128)(2,1)} %get-tuple-element.34), channel_id=1, source_target_pairs={{0,4},{1,5},{2,6},{3,7},{4,0},{5,1},{6,2},{7,3},{8,12},{9,13},{10,... | collective-permute-start | bytes 1572872 | tf_op jit(solution)/shard_map/ppermute | solution.py:141
  27.1 24.2 %collective-permute-start.4 = (bf16[256,1024]{1,0:T(8,128)(2,1)}, bf16[256,1024]{1,0:T(8,128)(2,1)S(1)}, u32[]{:S(2)}, u32[]{:S(2)}) collective-permute-start(bf16[256,1024]{1,0:T(8,128)(2,1)} %get-tuple-element.34), channel_id=1, source_target_pairs={{0,8},{1,9},{2,10},{3,11},{4,12},{5,13},{6,14},{7,15},{8,0},{9,1},... | collective-permute-start | bytes 1572872 | tf_op jit(solution)/shard_map/ppermute | solution.py:141
  38.5 196.8 %collective-permute-start.21 = (bf16[1024,1024]{1,0:T(8,128)(2,1)}, bf16[1024,1024]{1,0:T(8,128)(2,1)}, u32[]{:S(2)}, u32[]{:S(2)}) collective-permute-start(bf16[1024,1024]{1,0:T(8,128)(2,1)} %get-tuple-element.22), channel_id=1, source_target_pairs={{0,2},{1,3},{2,0},{3,1},{4,6},{5,7},{6,4},{7,5},{8,10},{9,11},{10,... | collective-permute-start | bytes 6291464 | tf_op jit(solution)/shard_map/ppermute | solution.py:141
  40.1 196.2 %collective-permute-start.20 = (bf16[1024,1024]{1,0:T(8,128)(2,1)S(1)}, bf16[1024,1024]{1,0:T(8,128)(2,1)}, u32[]{:S(2)}, u32[]{:S(2)}) collective-permute-start(bf16[1024,1024]{1,0:T(8,128)(2,1)S(1)} %bitcast.43), channel_id=1, source_target_pairs={{0,2},{1,3},{2,0},{3,1},{4,6},{5,7},{6,4},{7,5},{8,10},{9,11},{10,... | collective-permute-start | bytes 6291464 | tf_op jit(solution)/shard_map/ppermute | solution.py:141
  40.6 102.9 %collective-permute-start.1 = (bf16[256,1024]{1,0:T(8,128)(2,1)}, bf16[256,1024]{1,0:T(8,128)(2,1)S(1)}, u32[]{:S(2)}, u32[]{:S(2)}) collective-permute-start(bf16[256,1024]{1,0:T(8,128)(2,1)} %get-tuple-element.34), channel_id=1, source_target_pairs={{0,2},{1,3},{2,0},{3,1},{4,6},{5,7},{6,4},{7,5},{8,10},{9,11},{10,... | collective-permute-start | bytes 1572872 | tf_op jit(solution)/shard_map/ppermute | solution.py:141
  49.2 105.4 %collective-permute-start.3 = (bf16[256,1024]{1,0:T(8,128)(2,1)S(1)}, bf16[256,1024]{1,0:T(8,128)(2,1)S(1)}, u32[]{:S(2)}, u32[]{:S(2)}) collective-permute-start(bf16[256,1024]{1,0:T(8,128)(2,1)S(1)} %collective-permute-done.2), channel_id=1, source_target_pairs={{0,2},{1,3},{2,0},{3,1},{4,6},{5,7},{6,4},{7,5},{8,10},{9,11},{10,... | collective-permute-start | bytes 1572872 | tf_op jit(solution)/shard_map/ppermute | solution.py:141
  51.3 113.6 %collective-permute-start.5 = (bf16[256,1024]{1,0:T(8,128)(2,1)S(1)}, bf16[256,1024]{1,0:T(8,128)(2,1)S(1)}, u32[]{:S(2)}, u32[]{:S(2)}) collective-permute-start(bf16[256,1024]{1,0:T(8,128)(2,1)S(1)} %collective-permute-done.4), channel_id=1, source_target_pairs={{0,2},{1,3},{2,0},{3,1},{4,6},{5,7},{6,4},{7,5},{8,10},{9,11},{10,... | collective-permute-start | bytes 1572872 | tf_op jit(solution)/shard_map/ppermute | solution.py:141
  143.4 21.4 %copy-start.4 = (bf16[256,1024]{1,0:T(8,128)(2,1)}, bf16[256,1024]{1,0:T(8,128)(2,1)S(1)}, u32[]{:S(2)}) copy-start(bf16[256,1024]{1,0:T(8,128)(2,1)S(1)} %collective-permute-done.1) | copy-start | bytes 1572868
  143.4 103.5 %collective-permute-start.16 = (bf16[1024,1024]{1,0:T(8,128)(2,1)S(1)}, bf16[1024,1024]{1,0:T(8,128)(2,1)}, u32[]{:S(2)}, u32[]{:S(2)}) collective-permute-start(bf16[1024,1024]{1,0:T(8,128)(2,1)S(1)} %bitcast.44), channel_id=1, source_target_pairs={{0,4},{1,5},{2,6},{3,7},{4,0},{5,1},{6,2},{7,3},{8,12},{9,13},{10,... | collective-permute-start | bytes 6291464 | tf_op jit(solution)/shard_map/ppermute | solution.py:141
  154.7 10.2 %copy-start.1 = (bf16[256,1024]{1,0:T(8,128)(2,1)}, bf16[256,1024]{1,0:T(8,128)(2,1)S(1)}, u32[]{:S(2)}) copy-start(bf16[256,1024]{1,0:T(8,128)(2,1)S(1)} %collective-permute-done.3) | copy-start | bytes 1572868
  154.7 92.8 %collective-permute-start.8 = (bf16[1024,1024]{1,0:T(8,128)(2,1)S(1)}, bf16[1024,1024]{1,0:T(8,128)(2,1)}, u32[]{:S(2)}, u32[]{:S(2)}) collective-permute-start(bf16[1024,1024]{1,0:T(8,128)(2,1)S(1)} %bitcast.45), channel_id=1, source_target_pairs={{1,9},{3,11},{5,13},{7,15},{8,0},{10,2},{12,4},{14,6},{17,25},{19,... | collective-permute-start | bytes 6291464 | tf_op jit(solution)/shard_map/ppermute | solution.py:141
  164.9 0.8 copy-start.2
  165.7 57.2 %collective-permute-start.6 = (bf16[256,1024]{1,0:T(8,128)(2,1)S(1)}, bf16[256,1024]{1,0:T(8,128)(2,1)}, u32[]{:S(2)}, u32[]{:S(2)}) collective-permute-start(bf16[256,1024]{1,0:T(8,128)(2,1)S(1)} %collective-permute-done.4), channel_id=1, source_target_pairs={{0,4},{1,5},{2,6},{3,7},{4,0},{5,1},{6,2},{7,3},{8,12},{9,13},{10,... | collective-permute-start | bytes 1572872 | tf_op jit(solution)/shard_map/ppermute | solution.py:141
  166.3 85.9 %copy-start.3 = (bf16[256,1024]{1,0:T(8,128)(2,1)S(1)}, bf16[256,1024]{1,0:T(8,128)(2,1)}, u32[]{:S(2)}) copy-start(bf16[256,1024]{1,0:T(8,128)(2,1)} %copy-done.2) | copy-start | bytes 1572868
  222.8 9.9 %collective-permute-start.7 = (bf16[256,1024]{1,0:T(8,128)(2,1)}, bf16[256,1024]{1,0:T(8,128)(2,1)S(1)}, u32[]{:S(2)}, u32[]{:S(2)}) collective-permute-start(bf16[256,1024]{1,0:T(8,128)(2,1)} %collective-permute-done.6), channel_id=1, source_target_pairs={{0,2},{1,3},{2,0},{3,1},{4,6},{5,7},{6,4},{7,5},{8,10},{9,11},{10,... | collective-permute-start | bytes 1572872 | tf_op jit(solution)/shard_map/ppermute | solution.py:141
  232.7 71.4 %collective-permute-start.19 = (bf16[1024,1024]{1,0:T(8,128)(2,1)}, bf16[1024,1024]{1,0:T(8,128)(2,1)}, u32[]{:S(2)}, u32[]{:S(2)}) collective-permute-start(bf16[1024,1024]{1,0:T(8,128)(2,1)} %get-tuple-element.28), channel_id=1, source_target_pairs={{0,4},{1,5},{2,6},{3,7},{4,0},{5,1},{6,2},{7,3},{8,12},{9,13},{10,... | collective-permute-start | bytes 6291464 | tf_op jit(solution)/shard_map/ppermute | solution.py:141
  235.3 136.2 %collective-permute-start.18 = (bf16[1024,1024]{1,0:T(8,128)(2,1)}, bf16[1024,1024]{1,0:T(8,128)(2,1)}, u32[]{:S(2)}, u32[]{:S(2)}) collective-permute-start(bf16[1024,1024]{1,0:T(8,128)(2,1)} %get-tuple-element.23), channel_id=1, source_target_pairs={{0,6},{1,7},{2,4},{3,5},{4,2},{5,3},{6,0},{7,1},{8,14},{9,15},{10,... | collective-permute-start | bytes 6291464 | tf_op jit(solution)/shard_map/ppermute | solution.py:141
  236.2 140.8 %collective-permute-start.15 = (bf16[1024,1024]{1,0:T(8,128)(2,1)}, bf16[1024,1024]{1,0:T(8,128)(2,1)}, u32[]{:S(2)}, u32[]{:S(2)}) collective-permute-start(bf16[1024,1024]{1,0:T(8,128)(2,1)} %get-tuple-element.24), channel_id=1, source_target_pairs={{1,9},{3,11},{5,13},{7,15},{8,0},{10,2},{12,4},{14,6},{17,25},{19,... | collective-permute-start | bytes 6291464 | tf_op jit(solution)/shard_map/ppermute | solution.py:141
  246.9 141.7 %collective-permute-start.17 = (bf16[1024,1024]{1,0:T(8,128)(2,1)}, bf16[1024,1024]{1,0:T(8,128)(2,1)}, u32[]{:S(2)}, u32[]{:S(2)}) collective-permute-start(bf16[1024,1024]{1,0:T(8,128)(2,1)} %collective-permute-done.16.right), channel_id=1, source_target_pairs={{0,2},{1,3},{2,0},{3,1},{4,6},{5,7},{6,4},{7,5},{8,10},{9,11},{10,... | collective-permute-start | bytes 6291464 | tf_op jit(solution)/shard_map/ppermute | solution.py:141
  247.5 143.8 %collective-permute-start.9 = (bf16[1024,1024]{1,0:T(8,128)(2,1)}, bf16[1024,1024]{1,0:T(8,128)(2,1)}, u32[]{:S(2)}, u32[]{:S(2)}) collective-permute-start(bf16[1024,1024]{1,0:T(8,128)(2,1)} %collective-permute-done.8.right), channel_id=1, source_target_pairs={{0,4},{2,6},{4,0},{6,2},{9,13},{11,15},{13,9},{15,11},{16,20},{18,... | collective-permute-start | bytes 6291464 | tf_op jit(solution)/shard_map/ppermute | solution.py:141
  262.8 116.2 %copy-start.5 = (bf16[1024,1024]{1,0:T(8,128)(2,1)}, bf16[1024,1024]{1,0:T(8,128)(2,1)S(1)}, u32[]{:S(2)}) copy-start(bf16[1024,1024]{1,0:T(8,128)(2,1)S(1)} %fusion.8) | copy-start | bytes 6291460
  304.1 127.5 %collective-permute-start.14 = (bf16[1024,1024]{1,0:T(8,128)(2,1)}, bf16[1024,1024]{1,0:T(8,128)(2,1)}, u32[]{:S(2)}, u32[]{:S(2)}) collective-permute-start(bf16[1024,1024]{1,0:T(8,128)(2,1)} %get-tuple-element.25), channel_id=1, source_target_pairs={{1,11},{3,9},{5,15},{7,13},{8,2},{10,0},{12,6},{14,4},{17,27},{19,... | collective-permute-start | bytes 6291464 | tf_op jit(solution)/shard_map/ppermute | solution.py:141
  371.5 197.0 %collective-permute-start.12 = (bf16[1024,1024]{1,0:T(8,128)(2,1)}, bf16[1024,1024]{1,0:T(8,128)(2,1)}, u32[]{:S(2)}, u32[]{:S(2)}) collective-permute-start(bf16[1024,1024]{1,0:T(8,128)(2,1)} %get-tuple-element.26), channel_id=1, source_target_pairs={{1,13},{3,15},{5,9},{7,11},{8,4},{10,6},{12,0},{14,2},{17,29},{19,... | collective-permute-start | bytes 6291464 | tf_op jit(solution)/shard_map/ppermute | solution.py:141
  377.0 55.9 %collective-permute-start.13 = (bf16[1024,1024]{1,0:T(8,128)(2,1)}, bf16[1024,1024]{1,0:T(8,128)(2,1)}, u32[]{:S(2)}, u32[]{:S(2)}) collective-permute-start(bf16[1024,1024]{1,0:T(8,128)(2,1)} %collective-permute-done.8.right), channel_id=1, source_target_pairs={{0,2},{2,0},{4,6},{6,4},{9,11},{11,9},{13,15},{15,13},{16,18},{18,... | collective-permute-start | bytes 6291464 | tf_op jit(solution)/shard_map/ppermute | solution.py:141
  388.6 224.8 %collective-permute-start.11 = (bf16[1024,1024]{1,0:T(8,128)(2,1)}, bf16[1024,1024]{1,0:T(8,128)(2,1)}, u32[]{:S(2)}, u32[]{:S(2)}) collective-permute-start(bf16[1024,1024]{1,0:T(8,128)(2,1)} %get-tuple-element.27), channel_id=1, source_target_pairs={{1,15},{3,13},{5,11},{7,9},{8,6},{10,4},{12,2},{14,0},{17,31},{19,... | collective-permute-start | bytes 6291464 | tf_op jit(solution)/shard_map/ppermute | solution.py:141
  391.3 222.1 %collective-permute-start.10 = (bf16[1024,1024]{1,0:T(8,128)(2,1)}, bf16[1024,1024]{1,0:T(8,128)(2,1)}, u32[]{:S(2)}, u32[]{:S(2)}) collective-permute-start(bf16[1024,1024]{1,0:T(8,128)(2,1)} %collective-permute-done.9.right), channel_id=1, source_target_pairs={{0,2},{2,0},{4,6},{6,4},{9,11},{11,9},{13,15},{15,13},{16,18},{18,... | collective-permute-start | bytes 6291464 | tf_op jit(solution)/shard_map/ppermute | solution.py:141
  431.6 193.9 %collective-permute-start.25 = (bf16[1024,1024]{1,0:T(8,128)(2,1)S(1)}, bf16[1024,1024]{1,0:T(8,128)(2,1)S(1)}, u32[]{:S(2)}, u32[]{:S(2)}) collective-permute-start(bf16[1024,1024]{1,0:T(8,128)(2,1)S(1)} %get-tuple-element.16), channel_id=1, source_target_pairs={{0,8},{2,10},{4,12},{6,14},{9,1},{11,3},{13,5},{15,7},{16,24},{18,... | collective-permute-start | bytes 6291464 | tf_op jit(solution)/shard_map/ppermute | solution.py:141
  439.6 190.2 %collective-permute-start.24 = (bf16[1024,1024]{1,0:T(8,128)(2,1)S(1)}, bf16[1024,1024]{1,0:T(8,128)(2,1)S(1)}, u32[]{:S(2)}, u32[]{:S(2)}) collective-permute-start(bf16[1024,1024]{1,0:T(8,128)(2,1)S(1)} %get-tuple-element.15), channel_id=1, source_target_pairs={{0,10},{2,8},{4,14},{6,12},{9,3},{11,1},{13,7},{15,5},{16,26},{18,... | collective-permute-start | bytes 6291464 | tf_op jit(solution)/shard_map/ppermute | solution.py:141
  575.6 69.0 %collective-permute-start.23 = (bf16[1024,1024]{1,0:T(8,128)(2,1)}, bf16[1024,1024]{1,0:T(8,128)(2,1)S(1)}, u32[]{:S(2)}, u32[]{:S(2)}) collective-permute-start(bf16[1024,1024]{1,0:T(8,128)(2,1)} %get-tuple-element.14), channel_id=1, source_target_pairs={{0,12},{2,14},{4,8},{6,10},{9,5},{11,7},{13,1},{15,3},{16,28},{18,... | collective-permute-start | bytes 6291464 | tf_op jit(solution)/shard_map/ppermute | solution.py:141
  620.1 47.9 %collective-permute-start.22 = (bf16[1024,1024]{1,0:T(8,128)(2,1)S(1)}, bf16[1024,1024]{1,0:T(8,128)(2,1)S(1)}, u32[]{:S(2)}, u32[]{:S(2)}) collective-permute-start(bf16[1024,1024]{1,0:T(8,128)(2,1)S(1)} %get-tuple-element.13), channel_id=1, source_target_pairs={{0,14},{2,12},{4,10},{6,8},{9,7},{11,5},{13,3},{15,1},{16,30},{18,... | collective-permute-start | bytes 6291464 | tf_op jit(solution)/shard_map/ppermute | solution.py:141
